TPU v7x, 128 devices: a whole 4x4x4 slice. The times are simulated.
128 devices in a mesh: front: 4 (over y), row: 8 (over z, x_lo), col: 4 (over x_hi, core).
Axes of the slice: x: 4 (x_hi: 2, x_lo: 2; x = x_hi * 2 + x_lo), y: 4, z: 4, core: 2. Of those that a mesh axis runs over, the one named last changes fastest.
Arguments:
- front_entries: bfloat16 [36864, 9216], P(('front', 'row'), 'col'), parts along dimension 0, as said below
- children: bfloat16 [8, 8192, 8192], P('front', 'row', 'col'), parts along dimension 0, as said below
- child_maps: int32 [8, 64], P('front'), parts along dimension 0, may hold values from 0 to 71, as said below
Outputs:
- factor: float32 [36864, 9216], P(('front', 'row'), 'col'), parts along dimension 0
There are 4 independent parts, one for each index of `front`. A program takes and returns all parts, laid end to end along the dimension named above; each array names one. Nothing has to cross between parts.
Inputs may be any that keep to these rules, and one draw needn't show every extreme that they name: `front_entries`: symmetric in natural order; the leading 256 x 256 block of the matrix assembled by the steps is positive definite. `children`: each child's matrix is symmetric in natural order. `child_maps`: the entries of one child are distinct. For each child, among its blocks k with k mod 8 = a, exactly 1 has a value v with v mod 8 = d, for every a and d; and among its blocks k with k mod 4 = a, exactly 4 have a value v with v mod 4 = d, for every a and d.
All inputs are finite; a program needn't handle non-finite values.
Results may differ from a plain program's by a relative error of at most 0.0003.
Values may be sent and summed in bfloat16 or wider, within the bound.
A program may use at most 128 MiB of HBM per device.

v0:
```python
import jax
import jax.numpy as jnp
from jax import lax
from jax.sharding import PartitionSpec as P

BLK = 128
SEP = 256


def broadcast(value, axis, source):
    kept = jnp.where(lax.axis_index(axis) == source, value, 0).astype(value.dtype)
    return lax.psum(kept, axis)


def arrivals(child_maps, axis_size, own_index, blocks):
    local_ids = jnp.arange(blocks, dtype=jnp.int32)
    source = jnp.arange(axis_size, dtype=jnp.int32)
    parents = child_maps[:, local_ids[None, :] * axis_size + source[:, None]]
    ranking = jnp.argsort(
        jnp.where(parents % axis_size == own_index, 0, 1) * blocks + local_ids, axis=2
    )
    chosen = jnp.take_along_axis(parents, ranking[:, :, : blocks // axis_size], axis=2)
    return (chosen // axis_size).reshape(parents.shape[0], -1)


def sending_order(child_maps, axis_size, own_index, blocks):
    local_ids = jnp.arange(blocks, dtype=jnp.int32)
    parents = child_maps[:, local_ids * axis_size + own_index]
    return jnp.argsort(parents % axis_size * blocks + local_ids[None, :], axis=1)


def shards(front_entries, children, child_maps):
    rows_axis = lax.axis_size("row")
    cols_axis = lax.axis_size("col")
    own_row = lax.axis_index("row")
    own_col = lax.axis_index("col")
    front_rows = front_entries.shape[0] // BLK
    front_cols = front_entries.shape[1] // BLK
    child_rows = children.shape[1] // BLK
    child_cols = children.shape[2] // BLK
    row_sends = child_rows // rows_axis
    col_sends = child_cols // cols_axis
    row_order = sending_order(child_maps, rows_axis, own_row, child_rows)
    col_order = sending_order(child_maps, cols_axis, own_col, child_cols)
    tile_grid = children.reshape(2, child_rows, BLK, child_cols, BLK)
    tile_grid = jnp.take_along_axis(tile_grid, row_order[:, :, None, None, None], axis=1)
    tile_grid = jnp.take_along_axis(tile_grid, col_order[:, None, None, :, None], axis=3)
    tile_grid = tile_grid.reshape(2, rows_axis, row_sends, BLK, cols_axis, col_sends, BLK)
    outgoing = tile_grid.transpose(0, 1, 4, 2, 3, 5, 6).reshape(
        2, rows_axis * cols_axis, row_sends, BLK, col_sends, BLK
    )
    incoming = lax.all_to_all(outgoing, ("row", "col"), split_axis=1, concat_axis=1, tiled=True)
    incoming = incoming.reshape(2, rows_axis, cols_axis, row_sends, BLK, col_sends, BLK)
    arrived = incoming.transpose(0, 1, 3, 4, 2, 5, 6)
    arrived = arrived.reshape(2, child_rows, BLK, child_cols, BLK)
    row_dest = arrivals(child_maps, rows_axis, own_row, child_rows)
    col_dest = arrivals(child_maps, cols_axis, own_col, child_cols)
    assembled = front_entries.astype(jnp.float32).reshape(front_rows, BLK, front_cols, BLK)
    for child_index in range(2):
        addend = arrived[child_index].transpose(0, 2, 1, 3).astype(jnp.float32)
        assembled = assembled.at[
            row_dest[child_index][:, None], :, col_dest[child_index][None, :], :
        ].add(addend)
    assembled = assembled.reshape(front_rows * BLK, front_cols * BLK)
    row_blocks = jnp.arange(front_rows, dtype=jnp.int32) * rows_axis + own_row
    col_blocks = jnp.arange(front_cols, dtype=jnp.int32) * cols_axis + own_col
    spread = rows_axis // cols_axis

    def eliminate(pivot_index, current_front):
        col_slot = pivot_index // cols_axis
        column = lax.dynamic_slice_in_dim(current_front, col_slot * BLK, BLK, 1)
        column = broadcast(column, "col", pivot_index % cols_axis)
        diag_block = lax.dynamic_slice_in_dim(column, pivot_index // rows_axis * BLK, BLK, 0)
        diag_block = broadcast(diag_block, "row", pivot_index % rows_axis)
        diag_factor = jnp.tril(jnp.linalg.cholesky(diag_block))
        solved = lax.linalg.triangular_solve(
            diag_factor, column, left_side=False, lower=True, transpose_a=True
        )
        panel_tiles = solved.reshape(front_rows, BLK, BLK)
        panel_tiles = jnp.where(
            (row_blocks == pivot_index)[:, None, None], diag_factor[None], panel_tiles
        )
        stored_col = jnp.where(
            (row_blocks >= pivot_index)[:, None, None], panel_tiles, 0.0
        ).reshape(front_rows * BLK, BLK)
        below_rows = jnp.where((row_blocks > pivot_index)[:, None, None], panel_tiles, 0.0).reshape(
            front_rows * BLK, BLK
        )
        received = [
            broadcast(below_rows, "row", own_col + offset * cols_axis).reshape(front_rows, BLK, BLK)
            for offset in range(spread)
        ]
        across_cols = jnp.stack(received, axis=1).reshape(front_cols * BLK, BLK)
        updated = current_front - lax.dot_general(
            below_rows,
            across_cols,
            (((1,), (1,)), ((), ())),
            precision=lax.Precision.HIGHEST,
            preferred_element_type=jnp.float32,
        )
        present = lax.dynamic_slice_in_dim(updated, col_slot * BLK, BLK, 1)
        column_new = jnp.where(own_col == pivot_index % cols_axis, stored_col, present)
        return lax.dynamic_update_slice_in_dim(updated, column_new, col_slot * BLK, 1)

    finished = lax.fori_loop(0, SEP // BLK, eliminate, assembled)
    upper_mask = (row_blocks < SEP // BLK)[:, None] & (col_blocks >= SEP // BLK)[None, :]
    finished = finished.reshape(front_rows, BLK, front_cols, BLK)
    finished = jnp.where(upper_mask[:, None, :, None], 0.0, finished)
    return finished.reshape(front_rows * BLK, front_cols * BLK)


def solution(mesh):
    in_specs = (P(("front", "row"), "col"), P("front", "row", "col"), P("front", None))
    out_specs = P(("front", "row"), "col")
    return jax.shard_map(shards, mesh=mesh, in_specs=in_specs, out_specs=out_specs, check_vma=False)
```

profile of v0, /device:TPU:0, one launch (start us, length us, event | category | flops | bytes accessed | tf_op | source)
XLA Modules:
  0.0 783.9 jit_solution(9959633989343557825)
XLA Ops:
  6.5 0.8 copy.77
  7.3 0.6 gather_fusion.3
  7.9 0.7 sort.71
  8.6 0.6 gather_fusion.2
  9.2 0.7 sort.70
  10.0 0.6 gather_fusion
  10.9 0.7 sort.68
  11.7 9.9 %copy.114 = bf16[256,8,16,128]{3,2,1,0:T(8,128)(2,1)} copy(bf16[256,8,16,128]{3,1,2,0:T(8,128)(2,1)} %bitcast.166) | data formatting | bytes 16777216
  22.0 8.3 %gather_fusion.6 = bf16[16,128,16,128]{3,2,1,0:T(8,128)(2,1)} fusion(bf16[2,8,128,16,128]{4,3,2,1,0:T(8,128)(2,1)} %bitcast.158, s32[16]{0:T(128)S(1)} %reshape.558), kind=kCustom, calls=%fused_computation.6 | custom fusion | bytes 16777344 | tf_op jit(solution)/shard_map/jit(take_along_axis)/gather | solution.py:46
  30.3 8.8 %copy_select_fusion = bf16[2,8,128,16,128]{4,2,3,1,0:T(8,128)(2,1)} fusion(bf16[2,8,128,16,128]{4,3,2,1,0:T(8,128)(2,1)} %bitcast.159, pred[2,8]{1,0:T(4,128)(4,1)S(1)} %copy.93), kind=kLoop, calls=%fused_computation.37 | loop fusion | flops 4194304 | bytes 16777232 | tf_op jit(solution)/shard_map/jit(take_along_axis)/select_n | solution.py:46
  39.1 8.6 %gather_fusion.7 = bf16[32,8,128,128]{3,2,1,0:T(8,128)(2,1)} fusion(bf16[2,8,128,16,128]{4,2,3,1,0:T(8,128)(2,1)} %copy_select_fusion, s32[32]{0:T(128)S(1)} %reshape.564), kind=kCustom, calls=%fused_computation.7 | custom fusion | bytes 16777472 | tf_op jit(solution)/shard_map/jit(take_along_axis)/gather | solution.py:47
  47.7 10.5 %copy.98 = bf16[2,8,128,16,128]{4,2,3,1,0:T(8,128)(2,1)} copy(bf16[2,8,128,16,128]{4,2,1,3,0:T(8,128)(2,1)} %bitcast.157) | data formatting | bytes 16777216 | tf_op jit(solution)/shard_map/jit(take_along_axis)/gather | solution.py:47
  58.3 7.7 broadcast_select_fusion.4
  66.0 10.5 %copy.99 = bf16[2,32,1,128,4,128]{5,3,4,2,0,1:T(8,128)(2,1)} copy(bf16[2,32,1,128,4,128]{5,3,4,2,1,0:T(8,128)(2,1)} %bitcast.161) | data formatting | bytes 16777216 | tf_op jit(solution)/shard_map/reshape | solution.py:49
  76.5 8.4 %all-to-all-start = ((bf16[2,32,1,128,4,128]{5,3,4,2,0,1:T(8,128)(2,1)}), bf16[2,32,1,128,4,128]{5,3,4,2,0,1:T(8,128)(2,1)}, u32[]{:S(2)}, u32[]{:S(2)}) async-start(bf16[2,32,1,128,4,128]{5,3,4,2,0,1:T(8,128)(2,1)} %copy.99), calls=%async_computation | async-start | bytes 16777216 | tf_op jit(solution)/shard_map/all_to_all | solution.py:52
  84.9 10.9 %reshape.509 = f32[9,128,18,128]{3,2,1,0:T(8,128)} reshape(bf16[1152,2304]{1,0:T(8,128)(2,1)} %param.5) | data formatting | bytes 15925248 | tf_op jit(solution)/shard_map/reshape | solution.py:58
  95.7 11.0 %copy.100 = f32[9,128,18,128]{3,1,2,0:T(8,128)} copy(f32[9,128,18,128]{3,2,1,0:T(8,128)} %reshape.509) | data formatting | bytes 21233664 | tf_op jit(solution)/shard_map/reshape | solution.py:58
  106.8 0.6 gather_fusion.1
  107.6 0.8 sort.69
  108.7 0.8 gather_fusion.5
  109.9 0.7 gather_fusion.4
  111.4 69.6 %all-to-all-done = bf16[2,32,1,128,4,128]{5,3,4,2,0,1:T(8,128)(2,1)} async-done(((bf16[2,32,1,128,4,128]{5,3,4,2,0,1:T(8,128)(2,1)}), bf16[2,32,1,128,4,128]{5,3,4,2,0,1:T(8,128)(2,1)}, u32[]{:S(2)}, u32[]{:S(2)}) %all-to-all-start) | async-done | bytes 8388640 | tf_op jit(solution)/shard_map/all_to_all | solution.py:52
  181.0 3.8 fusion.18
  184.8 4.3 convert.5
  189.1 4.3 convert.6
  193.4 27.2 %scatter_fusion = f32[9,128,18,128]{3,1,2,0:T(8,128)} fusion(f32[9,128,18,128]{3,1,2,0:T(8,128)} %copy.100, s32[128]{0:T(128)S(1)} %reshape.570, f32[128,128,128]{2,1,0:T(8,128)} %bitcast.155), kind=kCustom, calls=%fused_computation.8 | custom fusion | flops 2097152 | bytes 25166848 | tf_op jit(solution)/shard_map/scatter-add | solution.py:63
  220.6 27.4 %scatter_fusion.1 = f32[9,128,18,128]{3,1,2,0:T(8,128)} fusion(f32[9,128,18,128]{3,1,2,0:T(8,128)} %scatter_fusion, s32[128]{0:T(128)S(1)} %reshape.576, f32[128,128,128]{2,1,0:T(8,128)} %bitcast.156), kind=kCustom, calls=%fused_computation.9 | custom fusion | flops 2097152 | bytes 25166848 | tf_op jit(solution)/shard_map/scatter-add | solution.py:63
  248.0 15.3 %copy.102 = f32[9,128,18,128]{3,2,1,0:T(8,128)} copy(f32[9,128,18,128]{3,1,2,0:T(8,128)} %scatter_fusion.1) | data formatting | bytes 21233664 | tf_op jit(solution)/shard_map/scatter-add | solution.py:63
  263.4 11.7 %copy.119 = f32[144,8,18,128]{3,1,2,0:T(8,128)} copy(f32[144,8,18,128]{3,2,1,0:T(8,128)} %bitcast.154) | data formatting | bytes 21233664
  275.1 490.8 %while.17 = (s32[]{:T(128)}, f32[1152,2304]{1,0:T(8,128)}, s32[]{:T(128)}, s32[]{:T(128)}, s32[]{:T(128)}, /*index=5*/s32[]{:T(128)}, s32[]{:T(128)}, s32[]{:T(1...) while((s32[]{:T(128)}, f32[1152,2304]{1,0:T(8,128)}, ...), condition=%wide.region_13.14_spmd.clone, body=%wide.region_6.13_spmd.clone.sunk | while | flops 4307976192 | bytes 43714316 | solution.py:105
  275.3 1.9 dynamic-slice_select_fusion.4
  277.4 45.2 %all-reduce.7.cloned.1.call-done = f32[1152,128]{1,0:T(8,128)} async-done(((f32[1152,128]{1,0:T(8,128)}), f32[1152,128]{1,0:T(8,128)}) %all-reduce.7.cloned.1.call-update) | async-done | bytes 589840 | tf_op jit(solution)/shard_map/while/body/eval_jaxpr/psum | solution.py:12
  322.6 1.5 dynamic-slice_select_fusion.5
  324.1 73.2 %all-reduce.9.cloned.1.call-done = f32[128,128]{1,0:T(8,128)} async-done(((f32[128,128]{1,0:T(8,128)}), f32[128,128]{1,0:T(8,128)}) %all-reduce.9.cloned.1.call-update) | async-done | bytes 65552 | tf_op jit(solution)/shard_map/while/body/eval_jaxpr/psum | solution.py:12
  397.3 0.9 copy.121
  398.3 0.9 fusion.31
  399.1 11.7 %cholesky.64 = f32[128,128]{1,0:T(8,128)S(1)} custom-call(f32[128,128]{1,0:T(8,128)S(1)} %fusion.31), custom_call_target="Cholesky" | custom-call | tf_op jit(solution)/shard_map/while/body/eval_jaxpr/jit(cholesky)/cholesky | solution.py:75
  410.9 0.6 compare_reduce_fusion.2
  411.5 0.6 select_bitcast_fusion.2
  412.1 9.8 %custom-call.44 = f32[1,128,128]{1,2,0:T(8,128)S(1)} custom-call(f32[1,128,128]{2,1,0:T(8,128)S(1)} %get-tuple-element.255), custom_call_target="InvertDiagBlocksLowerTriangular" | custom-call | tf_op jit(solution)/shard_map/while/body/eval_jaxpr/triangular_solve | solution.py:76
  421.9 1.7 broadcast_select_fusion.7
  423.6 1.1 broadcast_select_fusion.8
  424.7 80.9 %all-reduce.11.cloned.1.call-done = (f32[9,1,128,128]{3,2,1,0:T(8,128)}, f32[9,1,128,128]{3,2,1,0:T(8,128)}) async-done(((f32[9,1,128,128]{3,2,1,0:T(8,128)}, f32[9,1,128,128]{3,2,1,0:T(8,128)}), (f32[9,1,128,128]{3,2,1,0:T(8,128)}, f32[9,1,128,128]{3,2,1,0:T(8,128)})) %all-reduce.11.cloned.1.call-update) | async-done | bytes 1179664 | tf_op jit(solution)/shard_map/while/body/eval_jaxpr/psum | solution.py:12
  505.6 1.3 pad_maximum_fusion.2
  506.9 13.0 %convolution_subtract_fusion.2 = f32[1152,2304]{1,0:T(8,128)} fusion(f32[1152,2304]{1,0:T(8,128)} %get-tuple-element.284, f32[1152,128]{1,0:T(8,128)S(1)} %bitcast.150, f32[2304,128]{1,0:T(8,128)S(1)} %bitcast.151), kind=kOutput, calls=%fused_computation.11.clone.1 | convolution fusion | flops 4079517696 | bytes 23003136 | tf_op jit(solution)/shard_map/while/body/eval_jaxpr/dot_general | solution.py:94
  519.9 1.9 constant_dynamic-update-slice_fusion.2
  521.9 1.9 dynamic-slice_select_fusion.4
  523.9 42.7 %all-reduce.7.cloned.1.call-done = f32[1152,128]{1,0:T(8,128)} async-done(((f32[1152,128]{1,0:T(8,128)}), f32[1152,128]{1,0:T(8,128)}) %all-reduce.7.cloned.1.call-update) | async-done | bytes 589840 | tf_op jit(solution)/shard_map/while/body/eval_jaxpr/psum | solution.py:12
  566.6 1.5 dynamic-slice_select_fusion.5
  568.2 73.1 %all-reduce.9.cloned.1.call-done = f32[128,128]{1,0:T(8,128)} async-done(((f32[128,128]{1,0:T(8,128)}), f32[128,128]{1,0:T(8,128)}) %all-reduce.9.cloned.1.call-update) | async-done | bytes 65552 | tf_op jit(solution)/shard_map/while/body/eval_jaxpr/psum | solution.py:12
  641.3 0.9 copy.121
  642.2 0.9 fusion.31
  643.0 11.7 %cholesky.64 = f32[128,128]{1,0:T(8,128)S(1)} custom-call(f32[128,128]{1,0:T(8,128)S(1)} %fusion.31), custom_call_target="Cholesky" | custom-call | tf_op jit(solution)/shard_map/while/body/eval_jaxpr/jit(cholesky)/cholesky | solution.py:75
  654.8 0.6 compare_reduce_fusion.2
  655.4 0.6 select_bitcast_fusion.2
  656.0 9.8 %custom-call.44 = f32[1,128,128]{1,2,0:T(8,128)S(1)} custom-call(f32[1,128,128]{2,1,0:T(8,128)S(1)} %get-tuple-element.255), custom_call_target="InvertDiagBlocksLowerTriangular" | custom-call | tf_op jit(solution)/shard_map/while/body/eval_jaxpr/triangular_solve | solution.py:76
  665.8 1.7 broadcast_select_fusion.7
  667.5 1.1 broadcast_select_fusion.8
  668.7 80.8 %all-reduce.11.cloned.1.call-done = (f32[9,1,128,128]{3,2,1,0:T(8,128)}, f32[9,1,128,128]{3,2,1,0:T(8,128)}) async-done(((f32[9,1,128,128]{3,2,1,0:T(8,128)}, f32[9,1,128,128]{3,2,1,0:T(8,128)}), (f32[9,1,128,128]{3,2,1,0:T(8,128)}, f32[9,1,128,128]{3,2,1,0:T(8,128)})) %all-reduce.11.cloned.1.call-update) | async-done | bytes 1179664 | tf_op jit(solution)/shard_map/while/body/eval_jaxpr/psum | solution.py:12
  749.4 1.3 pad_maximum_fusion.2
  750.8 13.0 %convolution_subtract_fusion.2 = f32[1152,2304]{1,0:T(8,128)} fusion(f32[1152,2304]{1,0:T(8,128)} %get-tuple-element.284, f32[1152,128]{1,0:T(8,128)S(1)} %bitcast.150, f32[2304,128]{1,0:T(8,128)S(1)} %bitcast.151), kind=kOutput, calls=%fused_computation.11.clone.1 | convolution fusion | flops 4079517696 | bytes 23003136 | tf_op jit(solution)/shard_map/while/body/eval_jaxpr/dot_general | solution.py:94
  763.7 1.9 constant_dynamic-update-slice_fusion.2
  765.9 1.0 broadcast_in_dim.226
  766.9 9.9 %bitcast_select_fusion.1 = f32[1152,2304]{1,0:T(8,128)} fusion(f32[1152,2304]{1,0:T(8,128)} %get-tuple-element.166, pred[144,8,18,128]{3,2,1,0:T(8,128)(4,1)S(1)} %bitcast.165), kind=kLoop, calls=%fused_computation.36 | loop fusion | flops 2654208 | bytes 23887872 | tf_op jit(solution)/shard_map/jit(_where)/select_n | solution.py:108
  (87 shorter events, 3.1 us)
Async XLA Ops:
  76.5 104.5 %all-to-all-start = ((bf16[2,32,1,128,4,128]{5,3,4,2,0,1:T(8,128)(2,1)}), bf16[2,32,1,128,4,128]{5,3,4,2,0,1:T(8,128)(2,1)}, u32[]{:S(2)}, u32[]{:S(2)}) async-start(bf16[2,32,1,128,4,128]{5,3,4,2,0,1:T(8,128)(2,1)} %copy.99), calls=%async_computation | async-start | bytes 16777216 | tf_op jit(solution)/shard_map/all_to_all | solution.py:52
  275.3 47.3 %all-reduce.7.cloned.1.call-start = ((), (), s32[]{:S(2)}) async-start(), calls=%async_computation.1 | async-start | bytes 1179648 | tf_op jit(solution)/shard_map/while/body/eval_jaxpr/psum | solution.py:12
  277.3 120.1 %all-reduce.9.cloned.1.call-start = ((), (), s32[]{:S(2)}) async-start(), calls=%async_computation.2 | async-start | bytes 131072 | tf_op jit(solution)/shard_map/while/body/eval_jaxpr/psum | solution.py:12
  324.0 181.6 %all-reduce.11.cloned.1.call-start = ((), (), s32[]{:S(2)}) async-start(), calls=%async_computation.3 | async-start | bytes 2359296 | tf_op jit(solution)/shard_map/while/body/eval_jaxpr/psum | solution.py:12
  521.9 44.8 %all-reduce.7.cloned.1.call-start = ((), (), s32[]{:S(2)}) async-start(), calls=%async_computation.1 | async-start | bytes 1179648 | tf_op jit(solution)/shard_map/while/body/eval_jaxpr/psum | solution.py:12
  523.8 117.4 %all-reduce.9.cloned.1.call-start = ((), (), s32[]{:S(2)}) async-start(), calls=%async_computation.2 | async-start | bytes 131072 | tf_op jit(solution)/shard_map/while/body/eval_jaxpr/psum | solution.py:12
  568.1 181.3 %all-reduce.11.cloned.1.call-start = ((), (), s32[]{:S(2)}) async-start(), calls=%async_computation.3 | async-start | bytes 2359296 | tf_op jit(solution)/shard_map/while/body/eval_jaxpr/psum | solution.py:12
Sparse Core Ops, SparseCore 0:
  278.6 43.9 all-reduce.6
  325.0 72.2 all-reduce.8
  424.9 80.7 all-reduce.10
  524.9 41.6 all-reduce.6
  568.9 72.2 all-reduce.8
  668.8 80.5 all-reduce.10
where the time goes:
time: 794 us; the launch traced here: 784 us
  waiting for transfers between devices  466 us (59%)
  other arithmetic  156 us (20%)
  local copies, waits for them, and re-layouts  110 us (14%)
  matrix products  29.3 us (4%)
  between operations  13.9 us (2%)
  starting transfers between devices  8.58 us (1%)
    psum x6, waiting for transfers between devices, broadcast(): return lax.psum(kept, axis)  396 us
    all_to_all x1, waiting for transfers between devices, shards(): lax.all_to_all(outgoing, ('row', 'col'), split_axis=1, concat_axis=1, til...  69.6 us
    scatter-add x2, other arithmetic, shards(): assembled = assembled.at[row_dest[child_index][:, None], :, col_dest[chil...  54.6 us
    dot_general x2, matrix products, eliminate(): lax.dot_general(below_rows, across_cols, (((1,), (1,)), ((), ())), precis...  26 us
    another operation x6, other arithmetic, eliminate(): diag_factor = jnp.tril(jnp.linalg.cholesky(diag_block))  24.8 us
    unnamed x5, local copies, waits for them, and re-layouts  22.4 us
    reshape x2, local copies, waits for them, and re-layouts, shards(): front_entries.astype(jnp.float32).reshape(front_rows, BLK, front_cols, BLK)  21.8 us
    another operation x4, other arithmetic, eliminate(): lax.linalg.triangular_solve(diag_factor, column, left_side=False, lower=T...  20.8 us
  transfers between devices with their start and end apart: 7, of which 7 were waited for; matrix products, arithmetic and copies ran while one was open for 3% of the time, Pallas kernels for 0%

commit v1 on v0

--- a/solution.py
+++ b/solution.py
@@ -9,7 +9,13 @@
 
 def broadcast(value, axis, source):
     kept = jnp.where(lax.axis_index(axis) == source, value, 0).astype(value.dtype)
-    return lax.psum(kept, axis)
+
+    def detail_face(inputs):
+        oldest = lax.all_gather(inputs, axis_name=axis)
+        earlier = jnp.sum(oldest, axis=0)
+        return earlier
+
+    return detail_face(kept)
 
 
 def arrivals(child_maps, axis_size, own_index, blocks):

time: 794 us -> 921 us (1.16)
  waiting for transfers between devices: 466 us -> 527 us
  blocking collectives: 0 us -> 60.3 us
    all_gather x0 -> x6, waiting for transfers between devices: none -> 456 us  [detail_face(): oldest = lax.all_gather(inputs, axis_name=axis)]
    psum x6 -> x0, waiting for transfers between devices: 396 us -> none  [broadcast(): return lax.psum(kept, axis)]
    all_gather x0 -> x2, blocking collectives: none -> 60.3 us  [detail_face(): oldest = lax.all_gather(inputs, axis_name=axis)]
    reduce_sum x0 -> x8, other arithmetic: none -> 14.3 us  [detail_face(): earlier = jnp.sum(oldest, axis=0)]
where the time goes in v1:
time: 921 us; the launch traced here: 910 us
  waiting for transfers between devices  527 us (57%)
  other arithmetic  163 us (18%)
  local copies, waits for them, and re-layouts  108 us (12%)
  blocking collectives  60.3 us (7%)
  matrix products  28.8 us (3%)
  between operations  13.9 us (2%)
    all_gather x6, waiting for transfers between devices, detail_face(): oldest = lax.all_gather(inputs, axis_name=axis)  456 us
    all_to_all x1, waiting for transfers between devices, shards(): lax.all_to_all(outgoing, ('row', 'col'), split_axis=1, concat_axis=1, til...  69.6 us
    all_gather x2, blocking collectives, detail_face(): oldest = lax.all_gather(inputs, axis_name=axis)  60.3 us
    scatter-add x2, other arithmetic, shards(): assembled = assembled.at[row_dest[child_index][:, None], :, col_dest[chil...  54.6 us
    dot_general x2, matrix products, eliminate(): lax.dot_general(below_rows, across_cols, (((1,), (1,)), ((), ())), precis...  26 us
    another operation x6, other arithmetic, eliminate(): diag_factor = jnp.tril(jnp.linalg.cholesky(diag_block))  24.9 us
    unnamed x5, local copies, waits for them, and re-layouts  22.4 us
    reshape x2, local copies, waits for them, and re-layouts, shards(): front_entries.astype(jnp.float32).reshape(front_rows, BLK, front_cols, BLK)  21.8 us
  transfers between devices with their start and end apart: 7, of which 7 were waited for; matrix products, arithmetic and copies ran while one was open for 3% of the time, Pallas kernels for 0%

profile of v1, /device:TPU:0, one launch (start us, length us, event | category | flops | bytes accessed | tf_op | source)
XLA Modules:
  0.0 910.2 jit_solution(13669976361922222407)
XLA Ops:
  6.5 0.8 copy.71
  7.9 0.7 sort.71
  8.6 0.6 gather_fusion.2
  9.2 0.7 sort.70
  10.0 0.6 gather_fusion
  10.9 0.7 sort.68
  11.7 9.9 %copy.108 = bf16[256,8,16,128]{3,2,1,0:T(8,128)(2,1)} copy(bf16[256,8,16,128]{3,1,2,0:T(8,128)(2,1)} %bitcast.174) | data formatting | bytes 16777216
  22.0 8.3 gather_fusion.6
  30.3 8.8 copy_select_fusion
  39.1 8.6 gather_fusion.7
  47.7 10.5 %copy.92 = bf16[2,8,128,16,128]{4,2,3,1,0:T(8,128)(2,1)} copy(bf16[2,8,128,16,128]{4,2,1,3,0:T(8,128)(2,1)} %bitcast.166) | data formatting | bytes 16777216 | tf_op jit(solution)/shard_map/jit(take_along_axis)/gather | solution.py:53
  58.3 7.7 broadcast_select_fusion.4
  66.0 10.5 %copy.93 = bf16[2,32,1,128,4,128]{5,3,4,2,0,1:T(8,128)(2,1)} copy(bf16[2,32,1,128,4,128]{5,3,4,2,1,0:T(8,128)(2,1)} %bitcast.170) | data formatting | bytes 16777216 | tf_op jit(solution)/shard_map/reshape | solution.py:55
  76.5 8.4 all-to-all-start
  84.9 10.9 %reshape.547 = f32[9,128,18,128]{3,2,1,0:T(8,128)} reshape(bf16[1152,2304]{1,0:T(8,128)(2,1)} %param.5) | data formatting | bytes 15925248 | tf_op jit(solution)/shard_map/reshape | solution.py:64
  95.7 11.0 %copy.94 = f32[9,128,18,128]{3,1,2,0:T(8,128)} copy(f32[9,128,18,128]{3,2,1,0:T(8,128)} %reshape.547) | data formatting | bytes 21233664 | tf_op jit(solution)/shard_map/reshape | solution.py:64
  106.8 0.6 gather_fusion.1
  107.6 0.8 sort.69
  108.7 0.8 gather_fusion.5
  109.9 0.7 gather_fusion.4
  111.4 69.6 %all-to-all-done = bf16[2,32,1,128,4,128]{5,3,4,2,0,1:T(8,128)(2,1)} async-done(((bf16[2,32,1,128,4,128]{5,3,4,2,0,1:T(8,128)(2,1)}), bf16[2,32,1,128,4,128]{5,3,4,2,0,1:T(8,128)(2,1)}, u32[]{:S(2)}, u32[]{:S(2)}) %all-to-all-start) | async-done | bytes 8388640 | tf_op jit(solution)/shard_map/all_to_all | solution.py:58
  181.0 3.8 fusion.18
  184.8 4.3 convert.5
  189.1 4.3 convert.6
  193.4 27.2 %scatter_fusion = f32[9,128,18,128]{3,1,2,0:T(8,128)} fusion(f32[9,128,18,128]{3,1,2,0:T(8,128)} %copy.94, s32[128]{0:T(128)S(1)} %reshape.608, f32[128,128,128]{2,1,0:T(8,128)} %bitcast.164), kind=kCustom, calls=%fused_computation.8 | custom fusion | flops 2097152 | bytes 25166848 | tf_op jit(solution)/shard_map/scatter-add | solution.py:69
  220.6 27.4 %scatter_fusion.1 = f32[9,128,18,128]{3,1,2,0:T(8,128)} fusion(f32[9,128,18,128]{3,1,2,0:T(8,128)} %scatter_fusion, s32[128]{0:T(128)S(1)} %reshape.614, f32[128,128,128]{2,1,0:T(8,128)} %bitcast.165), kind=kCustom, calls=%fused_computation.9 | custom fusion | flops 2097152 | bytes 25166848 | tf_op jit(solution)/shard_map/scatter-add | solution.py:69
  248.0 15.3 %copy.96 = f32[9,128,18,128]{3,2,1,0:T(8,128)} copy(f32[9,128,18,128]{3,1,2,0:T(8,128)} %scatter_fusion.1) | data formatting | bytes 21233664 | tf_op jit(solution)/shard_map/scatter-add | solution.py:69
  263.4 11.7 %copy.113 = f32[144,8,18,128]{3,1,2,0:T(8,128)} copy(f32[144,8,18,128]{3,2,1,0:T(8,128)} %bitcast.162) | data formatting | bytes 21233664
  275.1 617.1 %while.17 = (s32[]{:T(128)}, f32[1152,2304]{1,0:T(8,128)}, s32[]{:T(128)}, s32[]{:T(128)}, s32[]{:T(128)}, /*index=5*/s32[]{:T(128)}, u32[]{:T(128)}, u32[]{:T(1...) while((s32[]{:T(128)}, f32[1152,2304]{1,0:T(8,128)}, ...), condition=%wide.region_13.14_spmd.clone, body=%wide.region_6.13_spmd.clone.sunk | while | flops 4310138880 | bytes 88147752 | solution.py:111
  275.3 1.9 dynamic-slice_select_fusion.4
  277.4 30.0 %all-gather.12.cloned.1.call-done = f32[4608,128]{1,0:T(8,128)} async-done(((f32[1152,128]{1,0:T(8,128)}), f32[4608,128]{1,0:T(8,128)}) %all-gather.12.cloned.1.call-update) | async-done | bytes 2359312 | tf_op jit(solution)/shard_map/while/body/eval_jaxpr/all_gather | solution.py:14
  307.4 1.9 reduce_sum.76
  309.3 30.2 %all-gather.7 = f32[1024,128]{1,0:T(8,128)S(1)} all-gather(f32[128,128]{1,0:T(8,128)S(1)} %dynamic-slice_select_fusion.5), channel_id=3, replica_groups=mesh['front'=4,'row'=8,'col'=4] {'row'}, dimensions={0}, use_global_device_ids=true | all-gather | bytes 589824 | tf_op jit(solution)/shard_map/while/body/eval_jaxpr/all_gather | solution.py:14
  339.6 11.7 %cholesky.64 = f32[128,128]{1,0:T(8,128)S(1)} custom-call(f32[128,128]{1,0:T(8,128)S(1)} %fusion.31), custom_call_target="Cholesky" | custom-call | tf_op jit(solution)/shard_map/while/body/eval_jaxpr/jit(cholesky)/cholesky | solution.py:81
  351.3 0.7 compare_reduce_fusion.2
  352.0 0.7 select_bitcast_fusion.2
  352.8 9.8 %custom-call.44 = f32[1,128,128]{1,2,0:T(8,128)S(1)} custom-call(f32[1,128,128]{2,1,0:T(8,128)S(1)} %get-tuple-element.249), custom_call_target="InvertDiagBlocksLowerTriangular" | custom-call | tf_op jit(solution)/shard_map/while/body/eval_jaxpr/triangular_solve | solution.py:82
  362.6 1.4 broadcast_select_fusion.8
  364.0 0.8 broadcast_select_fusion.9
  364.9 0.7 all-gather.16.cloned.1.call-update
  365.6 99.1 %all-gather.14.cloned.1.call-done = f32[8,1152,128]{2,1,0:T(8,128)} async-done(((f32[1,1152,128]{2,1,0:T(8,128)}), f32[8,1152,128]{2,1,0:T(8,128)}) %all-gather.14.cloned.1.call-update) | async-done | bytes 4718608 | tf_op jit(solution)/shard_map/while/body/eval_jaxpr/all_gather | solution.py:14
  464.7 2.6 reduce_sum.78
  467.3 99.6 %all-gather.16.cloned.1.call-done = f32[8,1152,128]{2,1,0:T(8,128)} async-done(((f32[1,1152,128]{2,1,0:T(8,128)}), f32[8,1152,128]{2,1,0:T(8,128)}) %all-gather.16.cloned.1.call-update) | async-done | bytes 4718608 | tf_op jit(solution)/shard_map/while/body/eval_jaxpr/all_gather | solution.py:14
  567.0 2.6 reduce_sum.79
  569.7 13.0 %convolution_subtract_fusion.2 = f32[1152,2304]{1,0:T(8,128)} fusion(f32[1152,2304]{1,0:T(8,128)} %get-tuple-element.276, f32[1152,128]{1,0:T(8,128)S(1)} %bitcast.154, f32[2304,128]{1,0:T(8,128)S(1)} %bitcast.155), kind=kOutput, calls=%fused_computation.11.clone.1 | convolution fusion | flops 4079517696 | bytes 23003136 | tf_op jit(solution)/shard_map/while/body/eval_jaxpr/dot_general | solution.py:100
  582.7 1.9 constant_dynamic-update-slice_fusion.2
  584.6 1.9 dynamic-slice_select_fusion.4
  586.7 28.2 %all-gather.12.cloned.1.call-done = f32[4608,128]{1,0:T(8,128)} async-done(((f32[1152,128]{1,0:T(8,128)}), f32[4608,128]{1,0:T(8,128)}) %all-gather.12.cloned.1.call-update) | async-done | bytes 2359312 | tf_op jit(solution)/shard_map/while/body/eval_jaxpr/all_gather | solution.py:14
  614.9 1.9 reduce_sum.76
  616.8 30.2 %all-gather.7 = f32[1024,128]{1,0:T(8,128)S(1)} all-gather(f32[128,128]{1,0:T(8,128)S(1)} %dynamic-slice_select_fusion.5), channel_id=3, replica_groups=mesh['front'=4,'row'=8,'col'=4] {'row'}, dimensions={0}, use_global_device_ids=true | all-gather | bytes 589824 | tf_op jit(solution)/shard_map/while/body/eval_jaxpr/all_gather | solution.py:14
  647.1 11.7 %cholesky.64 = f32[128,128]{1,0:T(8,128)S(1)} custom-call(f32[128,128]{1,0:T(8,128)S(1)} %fusion.31), custom_call_target="Cholesky" | custom-call | tf_op jit(solution)/shard_map/while/body/eval_jaxpr/jit(cholesky)/cholesky | solution.py:81
  658.8 0.7 compare_reduce_fusion.2
  659.5 0.7 select_bitcast_fusion.2
  660.3 9.8 %custom-call.44 = f32[1,128,128]{1,2,0:T(8,128)S(1)} custom-call(f32[1,128,128]{2,1,0:T(8,128)S(1)} %get-tuple-element.249), custom_call_target="InvertDiagBlocksLowerTriangular" | custom-call | tf_op jit(solution)/shard_map/while/body/eval_jaxpr/triangular_solve | solution.py:82
  670.1 1.4 broadcast_select_fusion.8
  671.5 0.8 broadcast_select_fusion.9
  673.0 99.2 %all-gather.14.cloned.1.call-done = f32[8,1152,128]{2,1,0:T(8,128)} async-done(((f32[1,1152,128]{2,1,0:T(8,128)}), f32[8,1152,128]{2,1,0:T(8,128)}) %all-gather.14.cloned.1.call-update) | async-done | bytes 4718608 | tf_op jit(solution)/shard_map/while/body/eval_jaxpr/all_gather | solution.py:14
  772.2 2.6 reduce_sum.78
  774.8 99.5 %all-gather.16.cloned.1.call-done = f32[8,1152,128]{2,1,0:T(8,128)} async-done(((f32[1,1152,128]{2,1,0:T(8,128)}), f32[8,1152,128]{2,1,0:T(8,128)}) %all-gather.16.cloned.1.call-update) | async-done | bytes 4718608 | tf_op jit(solution)/shard_map/while/body/eval_jaxpr/all_gather | solution.py:14
  874.3 2.6 reduce_sum.79
  877.0 13.0 %convolution_subtract_fusion.2 = f32[1152,2304]{1,0:T(8,128)} fusion(f32[1152,2304]{1,0:T(8,128)} %get-tuple-element.276, f32[1152,128]{1,0:T(8,128)S(1)} %bitcast.154, f32[2304,128]{1,0:T(8,128)S(1)} %bitcast.155), kind=kOutput, calls=%fused_computation.11.clone.1 | convolution fusion | flops 4079517696 | bytes 23003136 | tf_op jit(solution)/shard_map/while/body/eval_jaxpr/dot_general | solution.py:100
  890.0 1.9 constant_dynamic-update-slice_fusion.2
  892.2 1.0 broadcast_in_dim.226
  893.2 9.9 %bitcast_select_fusion.1 = f32[1152,2304]{1,0:T(8,128)} fusion(f32[1152,2304]{1,0:T(8,128)} %get-tuple-element.166, pred[144,8,18,128]{3,2,1,0:T(8,128)(4,1)S(1)} %bitcast.173), kind=kLoop, calls=%fused_computation.36 | loop fusion | flops 2654208 | bytes 23887872 | tf_op jit(solution)/shard_map/jit(_where)/select_n | solution.py:114
  (97 shorter events, 4.6 us)
Async XLA Ops:
  76.5 104.5 %all-to-all-start = ((bf16[2,32,1,128,4,128]{5,3,4,2,0,1:T(8,128)(2,1)}), bf16[2,32,1,128,4,128]{5,3,4,2,0,1:T(8,128)(2,1)}, u32[]{:S(2)}, u32[]{:S(2)}) async-start(bf16[2,32,1,128,4,128]{5,3,4,2,0,1:T(8,128)(2,1)} %copy.93), calls=%async_computation | async-start | bytes 16777216 | tf_op jit(solution)/shard_map/all_to_all | solution.py:58
  275.3 32.1 %all-gather.12.cloned.1.call-start = ((), (), s32[]{:S(2)}) async-start(), calls=%async_computation.1 | async-start | bytes 2949120 | tf_op jit(solution)/shard_map/while/body/eval_jaxpr/all_gather | solution.py:14
  277.3 187.4 %all-gather.14.cloned.1.call-start = ((), (), s32[]{:S(2)}) async-start(), calls=%async_computation.2 | async-start | bytes 5308416 | tf_op jit(solution)/shard_map/while/body/eval_jaxpr/all_gather | solution.py:14
  364.9 202.1 %all-gather.16.cloned.1.call-start = ((), (), s32[]{:S(2)}) async-start(), calls=%async_computation.3 | async-start | bytes 5308416 | tf_op jit(solution)/shard_map/while/body/eval_jaxpr/all_gather | solution.py:14
  584.6 30.3 %all-gather.12.cloned.1.call-start = ((), (), s32[]{:S(2)}) async-start(), calls=%async_computation.1 | async-start | bytes 2949120 | tf_op jit(solution)/shard_map/while/body/eval_jaxpr/all_gather | solution.py:14
  586.5 185.6 %all-gather.14.cloned.1.call-start = ((), (), s32[]{:S(2)}) async-start(), calls=%async_computation.2 | async-start | bytes 5308416 | tf_op jit(solution)/shard_map/while/body/eval_jaxpr/all_gather | solution.py:14
  672.4 201.9 %all-gather.16.cloned.1.call-start = ((), (), s32[]{:S(2)}) async-start(), calls=%async_computation.3 | async-start | bytes 5308416 | tf_op jit(solution)/shard_map/while/body/eval_jaxpr/all_gather | solution.py:14
Sparse Core Ops, SparseCore 0:
  277.8 29.5 all-gather.11
  365.0 99.6 all-gather.13
  466.3 100.5 all-gather.15
  586.8 28.0 all-gather.11
  672.5 99.6 all-gather.13
  773.7 100.5 all-gather.15
